TPU v7x, 32 devices: a whole 2x2x4 slice. The times are simulated.
32 devices in a mesh: grp: 4 (over z), gx: 2 (over y), gy: 4 (over x, core).
Axes of the slice: x: 2, y: 2, z: 4, core: 2. Of those that a mesh axis runs over, the one named last changes fastest.
Arguments:
- checkpoint: float32 [2, 2, 2, 32, 64, 256], P(None, None, None, 'gx', 'gy'), may hold values from -6 to 6
- courant: float32 [32, 64, 256], P('gx', 'gy'), may hold values from 0.03 to 0.15
- epsilon: float32 [32, 64, 256], P('gx', 'gy'), may hold values from 0.3 to 0.6
- delta: float32 [32, 64, 256], P('gx', 'gy'), may hold values from 0.05 to 0.3
- positions: int32 [4, 3, 512], replicated, may hold values from 0 to 255, as said below
- amplitudes: float32 [4, 16, 512], replicated, may hold values from -6 to 6
- offsets: int32 [16], replicated, may hold values from -8 to 8, as said below
Outputs:
- image: float32 [16, 32, 64, 256], P('grp', 'gx', 'gy')
Inputs may be any that keep to these rules, and one draw needn't show every extreme that they name: `positions`: each column of a row is a cell inside the grid: x below 32, y below 64, z below 256. `offsets`: both -8 and 8 occur.
All inputs are finite; a program needn't handle non-finite values.
Results may differ from a plain program's by a relative error of at most 0.0003.
Values sent between devices are 32-bit elements; how exact they have to be, the bound alone decides.
A program may use at most 128 MiB of HBM per device.

v0:
```python
import jax
import jax.numpy as jnp
from jax import lax
from jax.sharding import PartitionSpec as P

NSTEPS = 16
SNAP = 4
HMAX = 8


def with_halo(array, sides, width):
    for axis, dim in sides:
        count, length = (lax.axis_size(axis), array.shape[dim])
        up = [(i, (i + 1) % count) for i in range(count - 1)]
        down = [(j, i) for i, j in up]
        last = lax.slice_in_dim(array, length - width, length, axis=dim)
        leading = lax.slice_in_dim(array, 0, width, axis=dim)
        before = lax.ppermute(last, axis, up)
        after = lax.ppermute(leading, axis, down)
        array = jnp.concatenate([before, array, after], axis=dim)
    return array


def swapped(array, axis, stride):
    return lax.ppermute(array, axis, [(i, i ^ 1 << stride) for i in range(lax.axis_size(axis))])


def trim(array, layers):
    return array[..., layers : array.shape[-3] - layers, layers : array.shape[-2] - layers, :]


def advance(current_ext, previous, coefs, source, inside):
    main_ext = current_ext[:, 0]
    aux_ext = current_ext[:, 1]
    main_mid = main_ext[:, 1:-1, 1:-1]
    aux_mid = aux_ext[:, 1:-1, 1:-1]
    across = (
        main_ext[:, 2:, 1:-1]
        + main_ext[:, :-2, 1:-1]
        + main_ext[:, 1:-1, 2:]
        + main_ext[:, 1:-1, :-2]
        - 4.0 * main_mid
    )
    deep_pad = jnp.pad(aux_mid, ((0, 0), (0, 0), (0, 0), (1, 1)))
    vertical = deep_pad[..., 2:] + deep_pad[..., :-2] - 2.0 * aux_mid
    main_next = 2.0 * main_mid - previous[:, 0] + coefs[0] * across + coefs[1] * vertical + source
    aux_next = 2.0 * aux_mid - previous[:, 1] + coefs[1] * across + coefs[2] * vertical + source
    return jnp.stack([main_next, aux_next], 1) * inside


def image_block(pair_ext, shift_list, tile_x):

    def one_offset(shift):
        shifted_source = lax.dynamic_slice_in_dim(pair_ext[0], HMAX - shift, tile_x, 0)
        shifted_recv = lax.dynamic_slice_in_dim(pair_ext[1], HMAX + shift, tile_x, 0)
        return shifted_source * shifted_recv

    return jax.vmap(one_offset)(shift_list)


def shards(checkpoint, courant, epsilon, delta, positions, amplitudes, offsets):
    group_index = lax.axis_index("grp")
    tile_x, tile_y, depth = courant.shape
    full_x = tile_x * lax.axis_size("gx")
    full_y = tile_y * lax.axis_size("gy")
    anchor_x = lax.axis_index("gx") * tile_x
    anchor_y = lax.axis_index("gy") * tile_y
    total_offsets = offsets.shape[0]
    coefs = jnp.stack(
        [courant + 2.0 * courant * epsilon, courant * jnp.sqrt(2.0 * delta + 1.0), courant]
    )
    coef_full = with_halo(coefs, (("gx", 1), ("gy", 2)), SNAP - 1)
    shot_index = group_index // 2
    parity = group_index % 2
    is_source = parity == 0
    shot_state = lax.dynamic_index_in_dim(checkpoint, shot_index, 0, keepdims=False)
    own_current = jnp.where(is_source, shot_state[0], 0.0)
    own_previous = jnp.where(is_source, shot_state[1], 0.0)
    row_index = group_index[None]
    current = own_current[None]
    previous = own_previous[None]
    row_coords = positions[row_index]
    row_strengths = amplitudes[row_index]
    field_sets = row_coords.shape[0]
    half = total_offsets // 2
    image = jnp.zeros((half, tile_x, tile_y, depth), jnp.float32)
    for block in range(NSTEPS // SNAP):
        widened = with_halo(jnp.stack([current, previous]), (("gx", 3), ("gy", 4)), SNAP)
        current = widened[0]
        previous = widened[1]
        for substep in range(SNAP):
            extent = SNAP - 1 - substep
            moment = block * SNAP + substep
            cells_x = anchor_x - extent + jnp.arange(tile_x + 2 * extent)
            cells_y = anchor_y - extent + jnp.arange(tile_y + 2 * extent)
            valid_x = (cells_x >= 0) & (cells_x < full_x)
            valid_y = (cells_y >= 0) & (cells_y < full_y)
            span_x = tile_x + 2 * extent
            span_y = tile_y + 2 * extent
            local_x = row_coords[:, 0] - anchor_x + extent
            local_y = row_coords[:, 1] - anchor_y + extent
            local_z = row_coords[:, 2]
            valid = (local_x >= 0) & (local_x < span_x) & (local_y >= 0) & (local_y < span_y)
            set_index = jnp.arange(field_sets, dtype=jnp.int32)[:, None]
            flat_index = ((set_index * span_x + local_x) * span_y + local_y) * depth + local_z
            total_cells = field_sets * span_x * span_y * depth
            flat_index = jnp.where(valid, flat_index, total_cells)
            spread = (
                jnp.zeros((total_cells,), jnp.float32)
                .at[flat_index.ravel()]
                .add(row_strengths[:, moment].ravel(), mode="drop")
            )
            updated = advance(
                current,
                trim(previous, 1),
                trim(coef_full, SNAP - 1 - extent),
                spread.reshape(field_sets, span_x, span_y, depth),
                (valid_x[:, None, None] & valid_y[None, :, None]).astype(jnp.float32),
            )
            previous = trim(current, 1)
            current = updated
        own_main = current[0, 0]
        partner = swapped(own_main, "grp", 0)
        source_field = jnp.where(is_source, own_main, partner)
        recv_field = jnp.where(is_source, partner, own_main)
        pairs = jnp.stack([source_field, recv_field])[None]
        shift_list = lax.dynamic_slice_in_dim(offsets, parity * half, half)
        pairs_ext = with_halo(pairs, (("gx", 2),), HMAX)
        image = image + jnp.sum(
            jax.vmap(lambda single: image_block(single, shift_list, tile_x))(pairs_ext), axis=0
        )
    placed = jnp.zeros((total_offsets, tile_x, tile_y, depth), jnp.float32)
    image = lax.dynamic_update_slice_in_dim(placed, image, parity * half, 0)
    image = lax.psum_scatter(image, "grp", scatter_dimension=0, tiled=True)
    return image


def solution(mesh):
    return jax.shard_map(
        shards,
        mesh=mesh,
        in_specs=(
            P(None, None, None, "gx", "gy", None),
            P("gx", "gy", None),
            P("gx", "gy", None),
            P("gx", "gy", None),
            P(),
            P(),
            P(),
        ),
        out_specs=P("grp", "gx", "gy", None),
        check_vma=False,
    )
```

profile of v0, /device:TPU:0, one launch (start us, length us, event | category | flops | bytes accessed | tf_op | source)
XLA Modules:
  0.0 388.2 jit_solution(2590120977883109508)
XLA Ops:
  9.3 4.9 %collective-permute-start.4 = (f32[3,3,16,256]{3,2,1,0:T(8,128)}, f32[3,3,16,256]{3,2,1,0:T(8,128)S(1)}, u32[]{:S(2)}, u32[]{:S(2)}) collective-permute-start(f32[3,3,16,256]{3,2,1,0:T(8,128)} %get-tuple-element.129), channel_id=1, source_target_pairs={{0,4},{1,5},{2,6},{3,7},{8,12},{9,13},{10,14},{11,15},{16,20},{17,... | collective-permute-start | bytes 442376 | tf_op jit(solution)/shard_map/ppermute | solution.py:18
  17.7 4.6 %collective-permute-start = (f32[2,1,2,4,16,256]{5,4,3,2,1,0:T(8,128)}, f32[2,1,2,4,16,256]{5,4,3,2,1,0:T(8,128)S(1)}, u32[]{:S(2)}, u32[]{:S(2)}) collective-permute-start(f32[2,1,2,4,16,256]{5,4,3,2,1,0:T(8,128)} %get-tuple-element.111), channel_id=1, source_target_pairs={{0,4},{1,5},{2,6},{3,7},{8,12},{9,13},{10,14},{11,15},{16,20},{17,... | collective-permute-start | bytes 786440 | tf_op jit(solution)/shard_map/ppermute | solution.py:18
  27.1 3.3 scatter_custom_fusion.3
  31.2 3.3 scatter_custom_fusion.2
  35.4 3.3 scatter_custom_fusion.1
  39.6 3.4 scatter_custom_fusion
  46.9 4.7 %collective-permute-start.6 = (f32[3,22,3,256]{3,2,1,0:T(4,128)S(1)}, f32[3,22,3,256]{3,2,1,0:T(4,128)S(1)}, u32[]{:S(2)}, u32[]{:S(2)}) collective-permute-start(f32[3,22,3,256]{3,2,1,0:T(4,128)S(1)} %get-tuple-element.95), channel_id=1, source_target_pairs={{0,1},{1,2},{2,3},{4,5},{5,6},{6,7},{8,9},{9,10},{10,11},{12,13},{... | collective-permute-start | bytes 608264 | tf_op jit(solution)/shard_map/ppermute | solution.py:18
  53.5 2.8 collective-permute-done.7
  66.8 4.6 %collective-permute-start.11 = (f32[2,1,2,4,16,256]{5,4,3,2,1,0:T(8,128)S(1)}, f32[2,1,2,4,16,256]{5,4,3,2,1,0:T(8,128)S(1)}, u32[]{:S(2)}, u32[]{:S(2)}) collective-permute-start(f32[2,1,2,4,16,256]{5,4,3,2,1,0:T(8,128)S(1)} %get-tuple-element.109), channel_id=1, source_target_pairs={{0,4},{1,5},{2,6},{3,7},{8,12},{9,13},{10,14},{11,15},{16,20},{17,... | collective-permute-start | bytes 786440 | tf_op jit(solution)/shard_map/ppermute | solution.py:18
  72.6 2.6 collective-permute-done.11
  75.2 4.4 %collective-permute-done.12 = f32[2,1,2,4,16,256]{5,4,3,2,1,0:T(8,128)S(1)} collective-permute-done((f32[2,1,2,4,16,256]{5,4,3,2,1,0:T(8,128)S(1)}, f32[2,1,2,4,16,256]{5,4,3,2,1,0:T(8,128)S(1)}, u32[]{:S(2)}, u32[]{:S(2)}) %collective-permute-start.12) | collective-permute-done | bytes 262176 | tf_op jit(solution)/shard_map/ppermute | solution.py:19
  80.6 6.1 %collective-permute-start.13 = (f32[2,1,2,24,4,256]{5,4,3,2,1,0:T(4,128)}, f32[2,1,2,24,4,256]{5,4,3,2,1,0:T(4,128)}, u32[]{:S(2)}, u32[]{:S(2)}) collective-permute-start(f32[2,1,2,24,4,256]{5,4,3,2,1,0:T(4,128)} %get-tuple-element.75), channel_id=1, source_target_pairs={{0,1},{1,2},{2,3},{4,5},{5,6},{6,7},{8,9},{9,10},{10,11},{12,13},{... | collective-permute-start | bytes 1179656 | tf_op jit(solution)/shard_map/ppermute | solution.py:18
  88.0 4.1 %scatter_custom_fusion.7 = f32[65536]{0:T(1024)} fusion(s32[512]{0:T(512)S(1)} %bitcast.637, f32[512]{0:T(512)} %bitcast.651, f32[]{:T(128)} %constant.31.clone.1), kind=kCustom, calls=%fused_computation.502 | custom fusion | flops 512 | bytes 262656 | tf_op jit(solution)/shard_map/scatter-add | solution.py:111
  93.8 4.1 %scatter_custom_fusion.6 = f32[82944]{0:T(1024)} fusion(s32[512]{0:T(512)S(1)} %bitcast.633, f32[512]{0:T(512)} %bitcast.650, f32[]{:T(128)} %constant.31.clone.1), kind=kCustom, calls=%fused_computation.491 | custom fusion | flops 512 | bytes 332288 | tf_op jit(solution)/shard_map/scatter-add | solution.py:111
  99.8 4.1 %scatter_custom_fusion.5 = f32[102400]{0:T(1024)} fusion(s32[512]{0:T(512)S(1)} %bitcast.629, f32[512]{0:T(512)} %bitcast.649, f32[]{:T(128)} %constant.31.clone.1), kind=kCustom, calls=%fused_computation.483 | custom fusion | flops 512 | bytes 410112 | tf_op jit(solution)/shard_map/scatter-add | solution.py:111
  105.8 4.2 %scatter_custom_fusion.4 = f32[123904]{0:T(1024)} fusion(s32[512]{0:T(512)S(1)} %bitcast.625, f32[512]{0:T(512)S(1)} %bitcast.648, f32[]{:T(128)} %constant.31.clone.1), kind=kCustom, calls=%fused_computation.475 | custom fusion | flops 512 | bytes 495620 | tf_op jit(solution)/shard_map/scatter-add | solution.py:111
  110.0 2.0 reshape.1427
  125.4 5.2 %collective-permute-done.18 = f32[2,1,2,4,16,256]{5,4,3,2,1,0:T(8,128)S(1)} collective-permute-done((f32[2,1,2,4,16,256]{5,4,3,2,1,0:T(8,128)S(1)}, f32[2,1,2,4,16,256]{5,4,3,2,1,0:T(8,128)S(1)}, u32[]{:S(2)}, u32[]{:S(2)}) %collective-permute-start.18) | collective-permute-done | bytes 262176 | tf_op jit(solution)/shard_map/ppermute | solution.py:18
  130.7 4.4 %collective-permute-done.19 = f32[2,1,2,4,16,256]{5,4,3,2,1,0:T(8,128)S(1)} collective-permute-done((f32[2,1,2,4,16,256]{5,4,3,2,1,0:T(8,128)S(1)}, f32[2,1,2,4,16,256]{5,4,3,2,1,0:T(8,128)S(1)}, u32[]{:S(2)}, u32[]{:S(2)}) %collective-permute-start.19) | collective-permute-done | bytes 262176 | tf_op jit(solution)/shard_map/ppermute | solution.py:19
  136.1 2.7 collective-permute-start.20
  140.1 3.9 %scatter_custom_fusion.11 = f32[65536]{0:T(1024)} fusion(s32[512]{0:T(512)S(1)} %bitcast.638, f32[512]{0:T(512)S(1)} %bitcast.647, f32[]{:T(128)} %constant.31.clone.1), kind=kCustom, calls=%fused_computation.500 | custom fusion | flops 512 | bytes 262148 | tf_op jit(solution)/shard_map/scatter-add | solution.py:111
  145.7 4.0 %scatter_custom_fusion.10 = f32[82944]{0:T(1024)} fusion(s32[512]{0:T(512)S(1)} %bitcast.634, f32[512]{0:T(512)S(1)} %bitcast.646, f32[]{:T(128)} %constant.31.clone.1), kind=kCustom, calls=%fused_computation.489 | custom fusion | flops 512 | bytes 331780 | tf_op jit(solution)/shard_map/scatter-add | solution.py:111
  151.5 4.0 %scatter_custom_fusion.9 = f32[102400]{0:T(1024)} fusion(s32[512]{0:T(512)S(1)} %bitcast.630, f32[512]{0:T(512)S(1)} %bitcast.645, f32[]{:T(128)} %constant.31.clone.1), kind=kCustom, calls=%fused_computation.481 | custom fusion | flops 512 | bytes 409604 | tf_op jit(solution)/shard_map/scatter-add | solution.py:111
  157.4 4.2 %scatter_custom_fusion.8 = f32[123904]{0:T(1024)} fusion(s32[512]{0:T(512)S(1)} %bitcast.626, f32[512]{0:T(512)S(1)} %bitcast.644, f32[]{:T(128)} %constant.31.clone.1), kind=kCustom, calls=%fused_computation.473 | custom fusion | flops 512 | bytes 495620 | tf_op jit(solution)/shard_map/scatter-add | solution.py:111
  176.8 5.1 %collective-permute-done.25 = f32[2,1,2,4,16,256]{5,4,3,2,1,0:T(8,128)S(1)} collective-permute-done((f32[2,1,2,4,16,256]{5,4,3,2,1,0:T(8,128)S(1)}, f32[2,1,2,4,16,256]{5,4,3,2,1,0:T(8,128)S(1)}, u32[]{:S(2)}, u32[]{:S(2)}) %collective-permute-start.25) | collective-permute-done | bytes 262176 | tf_op jit(solution)/shard_map/ppermute | solution.py:18
  181.9 4.7 %collective-permute-done.26 = f32[2,1,2,4,16,256]{5,4,3,2,1,0:T(8,128)S(1)} collective-permute-done((f32[2,1,2,4,16,256]{5,4,3,2,1,0:T(8,128)S(1)}, f32[2,1,2,4,16,256]{5,4,3,2,1,0:T(8,128)S(1)}, u32[]{:S(2)}, u32[]{:S(2)}) %collective-permute-start.26) | collective-permute-done | bytes 262176 | tf_op jit(solution)/shard_map/ppermute | solution.py:19
  187.6 2.8 collective-permute-start.27
  191.7 3.9 %scatter_custom_fusion.15 = f32[65536]{0:T(1024)} fusion(s32[512]{0:T(512)S(1)} %bitcast.639, f32[512]{0:T(512)S(1)} %bitcast.643, f32[]{:T(128)} %constant.31.clone.1), kind=kCustom, calls=%fused_computation.498 | custom fusion | flops 512 | bytes 262148 | tf_op jit(solution)/shard_map/scatter-add | solution.py:111
  197.3 4.0 %scatter_custom_fusion.14 = f32[82944]{0:T(1024)} fusion(s32[512]{0:T(512)S(1)} %bitcast.635, f32[512]{0:T(512)S(1)} %bitcast.642, f32[]{:T(128)} %constant.31.clone.1), kind=kCustom, calls=%fused_computation.487 | custom fusion | flops 512 | bytes 331780 | tf_op jit(solution)/shard_map/scatter-add | solution.py:111
  203.1 4.0 %scatter_custom_fusion.13 = f32[102400]{0:T(1024)} fusion(s32[512]{0:T(512)S(1)} %bitcast.631, f32[512]{0:T(512)S(1)} %bitcast.641, f32[]{:T(128)} %constant.31.clone.1), kind=kCustom, calls=%fused_computation.479 | custom fusion | flops 512 | bytes 409604 | tf_op jit(solution)/shard_map/scatter-add | solution.py:111
  209.0 4.3 %scatter_custom_fusion.12 = f32[123904]{0:T(1024)} fusion(s32[512]{0:T(512)S(1)} %bitcast.627, f32[512]{0:T(512)S(1)} %bitcast.640, f32[]{:T(128)} %constant.31.clone.1), kind=kCustom, calls=%fused_computation.471 | custom fusion | flops 512 | bytes 495620 | tf_op jit(solution)/shard_map/scatter-add | solution.py:111
  230.2 4.9 %collective-permute-done.29 = f32[16,16,256]{2,1,0:T(8,128)S(1)} collective-permute-done((f32[16,16,256]{2,1,0:T(8,128)S(1)}, f32[16,16,256]{2,1,0:T(8,128)S(1)}, u32[]{:S(2)}, u32[]{:S(2)}) %collective-permute-start.29) | collective-permute-done | bytes 262176 | tf_op jit(solution)/shard_map/ppermute | solution.py:25
  238.0 13.9 %collective-permute-done.22 = f32[16,16,256]{2,1,0:T(8,128)S(1)} collective-permute-done((f32[16,16,256]{2,1,0:T(8,128)S(1)}, f32[16,16,256]{2,1,0:T(8,128)S(1)}, u32[]{:S(2)}, u32[]{:S(2)}) %collective-permute-start.22) | collective-permute-done | bytes 262176 | tf_op jit(solution)/shard_map/ppermute | solution.py:25
  255.0 4.6 %collective-permute-start.16 = (f32[1,2,8,16,256]{4,3,2,1,0:T(8,128)S(1)}, f32[1,2,8,16,256]{4,3,2,1,0:T(8,128)S(1)}, u32[]{:S(2)}, u32[]{:S(2)}) collective-permute-start(f32[1,2,8,16,256]{4,3,2,1,0:T(8,128)S(1)} %get-tuple-element.135), channel_id=1, source_target_pairs={{0,4},{1,5},{2,6},{3,7},{8,12},{9,13},{10,14},{11,15},{16,20},{17,... | collective-permute-start | bytes 786440 | tf_op jit(solution)/shard_map/ppermute | solution.py:18
  261.1 4.6 %collective-permute-start.9 = (f32[1,2,8,16,256]{4,3,2,1,0:T(8,128)S(1)}, f32[1,2,8,16,256]{4,3,2,1,0:T(8,128)S(1)}, u32[]{:S(2)}, u32[]{:S(2)}) collective-permute-start(f32[1,2,8,16,256]{4,3,2,1,0:T(8,128)S(1)} %get-tuple-element.131), channel_id=1, source_target_pairs={{0,4},{1,5},{2,6},{3,7},{8,12},{9,13},{10,14},{11,15},{16,20},{17,... | collective-permute-start | bytes 786440 | tf_op jit(solution)/shard_map/ppermute | solution.py:18
  267.3 2.1 collective-permute-done.17
  270.7 4.1 %collective-permute-done.10 = f32[1,2,8,16,256]{4,3,2,1,0:T(8,128)S(1)} collective-permute-done((f32[1,2,8,16,256]{4,3,2,1,0:T(8,128)S(1)}, f32[1,2,8,16,256]{4,3,2,1,0:T(8,128)S(1)}, u32[]{:S(2)}, u32[]{:S(2)}) %collective-permute-start.10) | collective-permute-done | bytes 262176 | tf_op jit(solution)/shard_map/ppermute | solution.py:19
  276.0 3.0 gather_fusion.1
  279.0 2.1 gather_fusion.3
  281.1 2.0 gather_fusion.5
  283.1 2.0 gather_fusion.7
  285.1 2.0 gather_fusion
  287.1 2.0 gather_fusion.2
  289.2 2.0 gather_fusion.4
  291.2 2.1 gather_fusion.6
  293.3 2.7 broadcast_in_dim.48
  297.0 7.5 %add_dynamic-update-slice_fusion = f32[16,16,16,256]{3,2,1,0:T(8,128)} fusion(f32[16,16,16,256]{3,2,1,0:T(8,128)} %broadcast_in_dim.48, s32[]{:T(128)S(6)} %select_n.223, f32[8,16,16,256]{3,2,1,0:T(8,128)} %gather_fusion.6, f32[8,16,16,256]{3,2,1,0:T(8,128)} %gather_fusion.7, f32[8,16,16,256]{3,2,1,0:T(8,128)} %gather_fusion.4, ...), kind=kLoop, calls=%fused_computation.28 | loop fusion | flops 3670016 | bytes 18874372 | tf_op jit(solution)/shard_map/dynamic_update_slice | solution.py:133
  304.5 76.4 %reduce-scatter.2.cloned.1.call-done = f32[4,16,16,256]{3,2,1,0:T(8,128)} async-done(((f32[16,16,16,256]{3,2,1,0:T(8,128)}), f32[4,16,16,256]{3,2,1,0:T(8,128)}) %reduce-scatter.2.cloned.1.call-update) | async-done | bytes 1048592 | tf_op jit(solution)/shard_map/reduce_scatter | solution.py:134
  (289 shorter events, 111.3 us)
Async XLA Ops:
  6.5 374.3 %reduce-scatter.2.cloned.1.call-start = ((), (), s32[]{:S(2)}) async-start(), calls=%async_computation.1 | async-start | bytes 5242880 | tf_op jit(solution)/shard_map/reduce_scatter | solution.py:134
  9.3 37.4 %collective-permute-start.4 = (f32[3,3,16,256]{3,2,1,0:T(8,128)}, f32[3,3,16,256]{3,2,1,0:T(8,128)S(1)}, u32[]{:S(2)}, u32[]{:S(2)}) collective-permute-start(f32[3,3,16,256]{3,2,1,0:T(8,128)} %get-tuple-element.129), channel_id=1, source_target_pairs={{0,4},{1,5},{2,6},{3,7},{8,12},{9,13},{10,14},{11,15},{16,20},{17,... | collective-permute-start | bytes 442376 | tf_op jit(solution)/shard_map/ppermute | solution.py:18
  14.2 32.5 %collective-permute-start.5 = (f32[3,3,16,256]{3,2,1,0:T(8,128)}, f32[3,3,16,256]{3,2,1,0:T(8,128)S(1)}, u32[]{:S(2)}, u32[]{:S(2)}) collective-permute-start(f32[3,3,16,256]{3,2,1,0:T(8,128)} %get-tuple-element.130), channel_id=1, source_target_pairs={{4,0},{5,1},{6,2},{7,3},{12,8},{13,9},{14,10},{15,11},{20,16},{21,... | collective-permute-start | bytes 442376 | tf_op jit(solution)/shard_map/ppermute | solution.py:19
  17.7 26.2 %collective-permute-start = (f32[2,1,2,4,16,256]{5,4,3,2,1,0:T(8,128)}, f32[2,1,2,4,16,256]{5,4,3,2,1,0:T(8,128)S(1)}, u32[]{:S(2)}, u32[]{:S(2)}) collective-permute-start(f32[2,1,2,4,16,256]{5,4,3,2,1,0:T(8,128)} %get-tuple-element.111), channel_id=1, source_target_pairs={{0,4},{1,5},{2,6},{3,7},{8,12},{9,13},{10,14},{11,15},{16,20},{17,... | collective-permute-start | bytes 786440 | tf_op jit(solution)/shard_map/ppermute | solution.py:18
  22.3 21.7 %collective-permute-start.1 = (f32[2,1,2,4,16,256]{5,4,3,2,1,0:T(8,128)}, f32[2,1,2,4,16,256]{5,4,3,2,1,0:T(8,128)S(1)}, u32[]{:S(2)}, u32[]{:S(2)}) collective-permute-start(f32[2,1,2,4,16,256]{5,4,3,2,1,0:T(8,128)} %get-tuple-element.112), channel_id=1, source_target_pairs={{4,0},{5,1},{6,2},{7,3},{12,8},{13,9},{14,10},{15,11},{20,16},{21,... | collective-permute-start | bytes 786440 | tf_op jit(solution)/shard_map/ppermute | solution.py:19
  43.0 3.8 copy-start
  43.9 2.9 copy-start.33
  44.0 2.9 copy-start.35
  44.1 13.5 %collective-permute-start.2 = (f32[2,1,2,24,4,256]{5,4,3,2,1,0:T(4,128)S(1)}, f32[2,1,2,24,4,256]{5,4,3,2,1,0:T(4,128)S(1)}, u32[]{:S(2)}, u32[]{:S(2)}) collective-permute-start(f32[2,1,2,24,4,256]{5,4,3,2,1,0:T(4,128)S(1)} %get-tuple-element.77), channel_id=1, source_target_pairs={{0,1},{1,2},{2,3},{4,5},{5,6},{6,7},{8,9},{9,10},{10,11},{12,13},{... | collective-permute-start | bytes 1179656 | tf_op jit(solution)/shard_map/ppermute | solution.py:18
  45.4 12.2 %collective-permute-start.3 = (f32[2,1,2,24,4,256]{5,4,3,2,1,0:T(4,128)S(1)}, f32[2,1,2,24,4,256]{5,4,3,2,1,0:T(4,128)S(1)}, u32[]{:S(2)}, u32[]{:S(2)}) collective-permute-start(f32[2,1,2,24,4,256]{5,4,3,2,1,0:T(4,128)S(1)} %get-tuple-element.78), channel_id=1, source_target_pairs={{1,0},{2,1},{3,2},{5,4},{6,5},{7,6},{9,8},{10,9},{11,10},{13,12},{... | collective-permute-start | bytes 1179656 | tf_op jit(solution)/shard_map/ppermute | solution.py:19
  46.7 6.8 %copy-start.43 = (f32[3,3,16,256]{3,2,1,0:T(8,128)}, f32[3,3,16,256]{3,2,1,0:T(8,128)S(1)}, u32[]{:S(2)}) copy-start(f32[3,3,16,256]{3,2,1,0:T(8,128)S(1)} %collective-permute-done.4) | copy-start | bytes 442372
  46.8 6.8 %copy-start.44 = (f32[3,3,16,256]{3,2,1,0:T(8,128)}, f32[3,3,16,256]{3,2,1,0:T(8,128)S(1)}, u32[]{:S(2)}) copy-start(f32[3,3,16,256]{3,2,1,0:T(8,128)S(1)} %collective-permute-done.5) | copy-start | bytes 442372
  46.9 6.6 %collective-permute-start.6 = (f32[3,22,3,256]{3,2,1,0:T(4,128)S(1)}, f32[3,22,3,256]{3,2,1,0:T(4,128)S(1)}, u32[]{:S(2)}, u32[]{:S(2)}) collective-permute-start(f32[3,22,3,256]{3,2,1,0:T(4,128)S(1)} %get-tuple-element.95), channel_id=1, source_target_pairs={{0,1},{1,2},{2,3},{4,5},{5,6},{6,7},{8,9},{9,10},{10,11},{12,13},{... | collective-permute-start | bytes 608264 | tf_op jit(solution)/shard_map/ppermute | solution.py:18
  51.7 4.7 %collective-permute-start.7 = (f32[3,22,3,256]{3,2,1,0:T(4,128)S(1)}, f32[3,22,3,256]{3,2,1,0:T(4,128)S(1)}, u32[]{:S(2)}, u32[]{:S(2)}) collective-permute-start(f32[3,22,3,256]{3,2,1,0:T(4,128)S(1)} %get-tuple-element.96), channel_id=1, source_target_pairs={{1,0},{2,1},{3,2},{5,4},{6,5},{7,6},{9,8},{10,9},{11,10},{13,12},{... | collective-permute-start | bytes 608264 | tf_op jit(solution)/shard_map/ppermute | solution.py:19
  53.5 4.1 %copy-start.34 = (f32[2,1,2,4,16,256]{5,4,3,2,1,0:T(8,128)S(1)}, f32[2,1,2,4,16,256]{5,4,3,2,1,0:T(8,128)}, u32[]{:S(2)}) copy-start(f32[2,1,2,4,16,256]{5,4,3,2,1,0:T(8,128)} %copy-done.33) | copy-start | bytes 786436
  53.5 4.1 %copy-start.36 = (f32[2,1,2,4,16,256]{5,4,3,2,1,0:T(8,128)S(1)}, f32[2,1,2,4,16,256]{5,4,3,2,1,0:T(8,128)}, u32[]{:S(2)}) copy-start(f32[2,1,2,4,16,256]{5,4,3,2,1,0:T(8,128)} %copy-done.35) | copy-start | bytes 786436
  66.8 8.4 %collective-permute-start.11 = (f32[2,1,2,4,16,256]{5,4,3,2,1,0:T(8,128)S(1)}, f32[2,1,2,4,16,256]{5,4,3,2,1,0:T(8,128)S(1)}, u32[]{:S(2)}, u32[]{:S(2)}) collective-permute-start(f32[2,1,2,4,16,256]{5,4,3,2,1,0:T(8,128)S(1)} %get-tuple-element.109), channel_id=1, source_target_pairs={{0,4},{1,5},{2,6},{3,7},{8,12},{9,13},{10,14},{11,15},{16,20},{17,... | collective-permute-start | bytes 786440 | tf_op jit(solution)/shard_map/ppermute | solution.py:18
  71.3 8.3 %collective-permute-start.12 = (f32[2,1,2,4,16,256]{5,4,3,2,1,0:T(8,128)S(1)}, f32[2,1,2,4,16,256]{5,4,3,2,1,0:T(8,128)S(1)}, u32[]{:S(2)}, u32[]{:S(2)}) collective-permute-start(f32[2,1,2,4,16,256]{5,4,3,2,1,0:T(8,128)S(1)} %get-tuple-element.110), channel_id=1, source_target_pairs={{4,0},{5,1},{6,2},{7,3},{12,8},{13,9},{14,10},{15,11},{20,16},{21,... | collective-permute-start | bytes 786440 | tf_op jit(solution)/shard_map/ppermute | solution.py:19
  75.2 4.4 %copy-start.39 = (f32[2,1,2,4,16,256]{5,4,3,2,1,0:T(8,128)}, f32[2,1,2,4,16,256]{5,4,3,2,1,0:T(8,128)S(1)}, u32[]{:S(2)}) copy-start(f32[2,1,2,4,16,256]{5,4,3,2,1,0:T(8,128)S(1)} %collective-permute-done.11) | copy-start | bytes 786436
  80.6 31.4 %collective-permute-start.13 = (f32[2,1,2,24,4,256]{5,4,3,2,1,0:T(4,128)}, f32[2,1,2,24,4,256]{5,4,3,2,1,0:T(4,128)}, u32[]{:S(2)}, u32[]{:S(2)}) collective-permute-start(f32[2,1,2,24,4,256]{5,4,3,2,1,0:T(4,128)} %get-tuple-element.75), channel_id=1, source_target_pairs={{0,1},{1,2},{2,3},{4,5},{5,6},{6,7},{8,9},{9,10},{10,11},{12,13},{... | collective-permute-start | bytes 1179656 | tf_op jit(solution)/shard_map/ppermute | solution.py:18
  86.7 25.3 %collective-permute-start.14 = (f32[2,1,2,24,4,256]{5,4,3,2,1,0:T(4,128)}, f32[2,1,2,24,4,256]{5,4,3,2,1,0:T(4,128)}, u32[]{:S(2)}, u32[]{:S(2)}) collective-permute-start(f32[2,1,2,24,4,256]{5,4,3,2,1,0:T(4,128)} %get-tuple-element.76), channel_id=1, source_target_pairs={{1,0},{2,1},{3,2},{5,4},{6,5},{7,6},{9,8},{10,9},{11,10},{13,12},{... | collective-permute-start | bytes 1179656 | tf_op jit(solution)/shard_map/ppermute | solution.py:19
  122.4 8.3 %collective-permute-start.18 = (f32[2,1,2,4,16,256]{5,4,3,2,1,0:T(8,128)S(1)}, f32[2,1,2,4,16,256]{5,4,3,2,1,0:T(8,128)S(1)}, u32[]{:S(2)}, u32[]{:S(2)}) collective-permute-start(f32[2,1,2,4,16,256]{5,4,3,2,1,0:T(8,128)S(1)} %get-tuple-element.107), channel_id=1, source_target_pairs={{0,4},{1,5},{2,6},{3,7},{8,12},{9,13},{10,14},{11,15},{16,20},{17,... | collective-permute-start | bytes 786440 | tf_op jit(solution)/shard_map/ppermute | solution.py:18
  124.1 11.0 %collective-permute-start.19 = (f32[2,1,2,4,16,256]{5,4,3,2,1,0:T(8,128)S(1)}, f32[2,1,2,4,16,256]{5,4,3,2,1,0:T(8,128)S(1)}, u32[]{:S(2)}, u32[]{:S(2)}) collective-permute-start(f32[2,1,2,4,16,256]{5,4,3,2,1,0:T(8,128)S(1)} %get-tuple-element.108), channel_id=1, source_target_pairs={{4,0},{5,1},{6,2},{7,3},{12,8},{13,9},{14,10},{15,11},{20,16},{21,... | collective-permute-start | bytes 786440 | tf_op jit(solution)/shard_map/ppermute | solution.py:19
  130.6 4.4 %copy-start.40 = (f32[2,1,2,4,16,256]{5,4,3,2,1,0:T(8,128)}, f32[2,1,2,4,16,256]{5,4,3,2,1,0:T(8,128)S(1)}, u32[]{:S(2)}) copy-start(f32[2,1,2,4,16,256]{5,4,3,2,1,0:T(8,128)S(1)} %collective-permute-done.18) | copy-start | bytes 786436
  136.1 27.5 %collective-permute-start.20 = (f32[2,1,2,24,4,256]{5,4,3,2,1,0:T(4,128)}, f32[2,1,2,24,4,256]{5,4,3,2,1,0:T(4,128)}, u32[]{:S(2)}, u32[]{:S(2)}) collective-permute-start(f32[2,1,2,24,4,256]{5,4,3,2,1,0:T(4,128)} %get-tuple-element.73), channel_id=1, source_target_pairs={{0,1},{1,2},{2,3},{4,5},{5,6},{6,7},{8,9},{9,10},{10,11},{12,13},{... | collective-permute-start | bytes 1179656 | tf_op jit(solution)/shard_map/ppermute | solution.py:18
  138.8 24.8 %collective-permute-start.21 = (f32[2,1,2,24,4,256]{5,4,3,2,1,0:T(4,128)}, f32[2,1,2,24,4,256]{5,4,3,2,1,0:T(4,128)}, u32[]{:S(2)}, u32[]{:S(2)}) collective-permute-start(f32[2,1,2,24,4,256]{5,4,3,2,1,0:T(4,128)} %get-tuple-element.74), channel_id=1, source_target_pairs={{1,0},{2,1},{3,2},{5,4},{6,5},{7,6},{9,8},{10,9},{11,10},{13,12},{... | collective-permute-start | bytes 1179656 | tf_op jit(solution)/shard_map/ppermute | solution.py:19
  174.0 7.8 %collective-permute-start.25 = (f32[2,1,2,4,16,256]{5,4,3,2,1,0:T(8,128)S(1)}, f32[2,1,2,4,16,256]{5,4,3,2,1,0:T(8,128)S(1)}, u32[]{:S(2)}, u32[]{:S(2)}) collective-permute-start(f32[2,1,2,4,16,256]{5,4,3,2,1,0:T(8,128)S(1)} %get-tuple-element.105), channel_id=1, source_target_pairs={{0,4},{1,5},{2,6},{3,7},{8,12},{9,13},{10,14},{11,15},{16,20},{17,... | collective-permute-start | bytes 786440 | tf_op jit(solution)/shard_map/ppermute | solution.py:18
  175.5 11.1 %collective-permute-start.26 = (f32[2,1,2,4,16,256]{5,4,3,2,1,0:T(8,128)S(1)}, f32[2,1,2,4,16,256]{5,4,3,2,1,0:T(8,128)S(1)}, u32[]{:S(2)}, u32[]{:S(2)}) collective-permute-start(f32[2,1,2,4,16,256]{5,4,3,2,1,0:T(8,128)S(1)} %get-tuple-element.106), channel_id=1, source_target_pairs={{4,0},{5,1},{6,2},{7,3},{12,8},{13,9},{14,10},{15,11},{20,16},{21,... | collective-permute-start | bytes 786440 | tf_op jit(solution)/shard_map/ppermute | solution.py:19
  181.9 4.7 %copy-start.37 = (f32[2,1,2,4,16,256]{5,4,3,2,1,0:T(8,128)}, f32[2,1,2,4,16,256]{5,4,3,2,1,0:T(8,128)S(1)}, u32[]{:S(2)}) copy-start(f32[2,1,2,4,16,256]{5,4,3,2,1,0:T(8,128)S(1)} %collective-permute-done.25) | copy-start | bytes 786436
  187.6 27.7 %collective-permute-start.27 = (f32[2,1,2,24,4,256]{5,4,3,2,1,0:T(4,128)}, f32[2,1,2,24,4,256]{5,4,3,2,1,0:T(4,128)}, u32[]{:S(2)}, u32[]{:S(2)}) collective-permute-start(f32[2,1,2,24,4,256]{5,4,3,2,1,0:T(4,128)} %get-tuple-element.71), channel_id=1, source_target_pairs={{0,1},{1,2},{2,3},{4,5},{5,6},{6,7},{8,9},{9,10},{10,11},{12,13},{... | collective-permute-start | bytes 1179656 | tf_op jit(solution)/shard_map/ppermute | solution.py:18
  190.4 24.9 %collective-permute-start.28 = (f32[2,1,2,24,4,256]{5,4,3,2,1,0:T(4,128)}, f32[2,1,2,24,4,256]{5,4,3,2,1,0:T(4,128)}, u32[]{:S(2)}, u32[]{:S(2)}) collective-permute-start(f32[2,1,2,24,4,256]{5,4,3,2,1,0:T(4,128)} %get-tuple-element.72), channel_id=1, source_target_pairs={{1,0},{2,1},{3,2},{5,4},{6,5},{7,6},{9,8},{10,9},{11,10},{13,12},{... | collective-permute-start | bytes 1179656 | tf_op jit(solution)/shard_map/ppermute | solution.py:19
  224.9 2.8 copy-start.45
  226.0 9.1 %collective-permute-start.29 = (f32[16,16,256]{2,1,0:T(8,128)S(1)}, f32[16,16,256]{2,1,0:T(8,128)S(1)}, u32[]{:S(2)}, u32[]{:S(2)}) collective-permute-start(f32[16,16,256]{2,1,0:T(8,128)S(1)} %get-tuple-element.171), channel_id=1, source_target_pairs={{0,8},{8,0},{16,24},{24,16},{1,9},{9,1},{17,25},{25,17},{2,10},{10... | collective-permute-start | bytes 786440 | tf_op jit(solution)/shard_map/ppermute | solution.py:25
  227.7 27.3 %collective-permute-start.8 = (f32[16,16,256]{2,1,0:T(8,128)S(1)}, f32[16,16,256]{2,1,0:T(8,128)S(1)}, u32[]{:S(2)}, u32[]{:S(2)}) collective-permute-start(f32[16,16,256]{2,1,0:T(8,128)S(1)} %get-tuple-element.168), channel_id=1, source_target_pairs={{0,8},{8,0},{16,24},{24,16},{1,9},{9,1},{17,25},{25,17},{2,10},{10... | collective-permute-start | bytes 786440 | tf_op jit(solution)/shard_map/ppermute | solution.py:25
  228.2 25.4 %collective-permute-start.15 = (f32[16,16,256]{2,1,0:T(8,128)S(1)}, f32[16,16,256]{2,1,0:T(8,128)S(1)}, u32[]{:S(2)}, u32[]{:S(2)}) collective-permute-start(f32[16,16,256]{2,1,0:T(8,128)S(1)} %get-tuple-element.169), channel_id=1, source_target_pairs={{0,8},{8,0},{16,24},{24,16},{1,9},{9,1},{17,25},{25,17},{2,10},{10... | collective-permute-start | bytes 786440 | tf_op jit(solution)/shard_map/ppermute | solution.py:25
  229.8 22.2 %collective-permute-start.22 = (f32[16,16,256]{2,1,0:T(8,128)S(1)}, f32[16,16,256]{2,1,0:T(8,128)S(1)}, u32[]{:S(2)}, u32[]{:S(2)}) collective-permute-start(f32[16,16,256]{2,1,0:T(8,128)S(1)} %get-tuple-element.170), channel_id=1, source_target_pairs={{0,8},{8,0},{16,24},{24,16},{1,9},{9,1},{17,25},{25,17},{2,10},{10... | collective-permute-start | bytes 786440 | tf_op jit(solution)/shard_map/ppermute | solution.py:25
  235.2 24.5 %collective-permute-start.30 = (f32[1,2,8,16,256]{4,3,2,1,0:T(8,128)S(1)}, f32[1,2,8,16,256]{4,3,2,1,0:T(8,128)S(1)}, u32[]{:S(2)}, u32[]{:S(2)}) collective-permute-start(f32[1,2,8,16,256]{4,3,2,1,0:T(8,128)S(1)} %get-tuple-element.143), channel_id=1, source_target_pairs={{0,4},{1,5},{2,6},{3,7},{8,12},{9,13},{10,14},{11,15},{16,20},{17,... | collective-permute-start | bytes 786440 | tf_op jit(solution)/shard_map/ppermute | solution.py:18
  236.7 24.4 %collective-permute-start.31 = (f32[1,2,8,16,256]{4,3,2,1,0:T(8,128)S(1)}, f32[1,2,8,16,256]{4,3,2,1,0:T(8,128)S(1)}, u32[]{:S(2)}, u32[]{:S(2)}) collective-permute-start(f32[1,2,8,16,256]{4,3,2,1,0:T(8,128)S(1)} %get-tuple-element.144), channel_id=1, source_target_pairs={{4,0},{5,1},{6,2},{7,3},{12,8},{13,9},{14,10},{15,11},{20,16},{21,... | collective-permute-start | bytes 786440 | tf_op jit(solution)/shard_map/ppermute | solution.py:19
  252.1 13.7 %collective-permute-start.23 = (f32[1,2,8,16,256]{4,3,2,1,0:T(8,128)S(1)}, f32[1,2,8,16,256]{4,3,2,1,0:T(8,128)S(1)}, u32[]{:S(2)}, u32[]{:S(2)}) collective-permute-start(f32[1,2,8,16,256]{4,3,2,1,0:T(8,128)S(1)} %get-tuple-element.139), channel_id=1, source_target_pairs={{0,4},{1,5},{2,6},{3,7},{8,12},{9,13},{10,14},{11,15},{16,20},{17,... | collective-permute-start | bytes 786440 | tf_op jit(solution)/shard_map/ppermute | solution.py:18
  253.6 13.5 %collective-permute-start.24 = (f32[1,2,8,16,256]{4,3,2,1,0:T(8,128)S(1)}, f32[1,2,8,16,256]{4,3,2,1,0:T(8,128)S(1)}, u32[]{:S(2)}, u32[]{:S(2)}) collective-permute-start(f32[1,2,8,16,256]{4,3,2,1,0:T(8,128)S(1)} %get-tuple-element.140), channel_id=1, source_target_pairs={{4,0},{5,1},{6,2},{7,3},{12,8},{13,9},{14,10},{15,11},{20,16},{21,... | collective-permute-start | bytes 786440 | tf_op jit(solution)/shard_map/ppermute | solution.py:19
  255.0 12.3 %collective-permute-start.16 = (f32[1,2,8,16,256]{4,3,2,1,0:T(8,128)S(1)}, f32[1,2,8,16,256]{4,3,2,1,0:T(8,128)S(1)}, u32[]{:S(2)}, u32[]{:S(2)}) collective-permute-start(f32[1,2,8,16,256]{4,3,2,1,0:T(8,128)S(1)} %get-tuple-element.135), channel_id=1, source_target_pairs={{0,4},{1,5},{2,6},{3,7},{8,12},{9,13},{10,14},{11,15},{16,20},{17,... | collective-permute-start | bytes 786440 | tf_op jit(solution)/shard_map/ppermute | solution.py:18
  259.8 9.6 %collective-permute-start.17 = (f32[1,2,8,16,256]{4,3,2,1,0:T(8,128)S(1)}, f32[1,2,8,16,256]{4,3,2,1,0:T(8,128)S(1)}, u32[]{:S(2)}, u32[]{:S(2)}) collective-permute-start(f32[1,2,8,16,256]{4,3,2,1,0:T(8,128)S(1)} %get-tuple-element.136), channel_id=1, source_target_pairs={{4,0},{5,1},{6,2},{7,3},{12,8},{13,9},{14,10},{15,11},{20,16},{21,... | collective-permute-start | bytes 786440 | tf_op jit(solution)/shard_map/ppermute | solution.py:19
  261.1 9.7 %collective-permute-start.9 = (f32[1,2,8,16,256]{4,3,2,1,0:T(8,128)S(1)}, f32[1,2,8,16,256]{4,3,2,1,0:T(8,128)S(1)}, u32[]{:S(2)}, u32[]{:S(2)}) collective-permute-start(f32[1,2,8,16,256]{4,3,2,1,0:T(8,128)S(1)} %get-tuple-element.131), channel_id=1, source_target_pairs={{0,4},{1,5},{2,6},{3,7},{8,12},{9,13},{10,14},{11,15},{16,20},{17,... | collective-permute-start | bytes 786440 | tf_op jit(solution)/shard_map/ppermute | solution.py:18
  265.8 9.1 %collective-permute-start.10 = (f32[1,2,8,16,256]{4,3,2,1,0:T(8,128)S(1)}, f32[1,2,8,16,256]{4,3,2,1,0:T(8,128)S(1)}, u32[]{:S(2)}, u32[]{:S(2)}) collective-permute-start(f32[1,2,8,16,256]{4,3,2,1,0:T(8,128)S(1)} %get-tuple-element.132), channel_id=1, source_target_pairs={{4,0},{5,1},{6,2},{7,3},{12,8},{13,9},{14,10},{15,11},{20,16},{21,... | collective-permute-start | bytes 786440 | tf_op jit(solution)/shard_map/ppermute | solution.py:19
  283.1 2.0 copy-start.1
  291.2 4.8 %copy-start.4 = (f32[8,16,16,256]{3,2,1,0:T(8,128)S(1)}, f32[8,16,16,256]{3,2,1,0:T(8,128)}, u32[]{:S(2)}) copy-start(f32[8,16,16,256]{3,2,1,0:T(8,128)} %gather_fusion.5) | copy-start | bytes 6291460
  293.3 2.7 copy-start.2
  293.3 3.7 copy-start.3
  (31 other events, 30.3 us)
Sparse Core Ops, SparseCore 0:
  304.6 76.1 reduce-scatter.1
where the time goes:
time: 396 us; the launch traced here: 388 us
  waiting for transfers between devices  132 us (33%)
  other arithmetic  103 us (26%)
  starting transfers between devices  69.5 us (18%)
  local copies, waits for them, and re-layouts  68.9 us (17%)
  between operations  15.3 us (4%)
    reduce_scatter x1, waiting for transfers between devices, shards(): image = lax.psum_scatter(image, 'grp', scatter_dimension=0, tiled=True)  76.4 us
    scatter-add x16, other arithmetic, shards(): spread = jnp.zeros((total_cells,), jnp.float32).at[flat_index.ravel()].ad...  62.1 us
    ppermute x14, starting transfers between devices, with_halo(): before = lax.ppermute(last, axis, up)  46.9 us
    reshape x16, local copies, waits for them, and re-layouts, shards(): spread.reshape(field_sets, span_x, span_y, depth)  25.8 us
    ppermute x14, waiting for transfers between devices, with_halo(): after = lax.ppermute(leading, axis, down)  22.6 us
    ppermute x4, waiting for transfers between devices, swapped(): lax.ppermute(array, axis, [(i, i ^ 1 << stride) for i in range(lax.axis_s...  18.8 us
    ppermute x14, starting transfers between devices, with_halo(): after = lax.ppermute(leading, axis, down)  18.5 us
    unnamed x92, local copies, waits for them, and re-layouts  17.5 us
  transfers between devices with their start and end apart: 33, of which 13 were waited for; matrix products, arithmetic and copies ran while one was open for 25% of the time, Pallas kernels for 0%

commit v1 on v0

v1 whole, which is shorter than its diff:
```python
import functools
import jax
import jax.numpy as jnp
from jax import lax
from jax.experimental import pallas as pl
from jax.experimental.pallas import tpu as pltpu
from jax.sharding import PartitionSpec as P

SNAP = 4
HMAX = 8
MESH = pl.DeviceIdType.MESH


def kernel(sizes, courant, epsilon, delta, checkpoint, positions, amplitudes, offsets, out,
           state, hor, cpl, ver, inj, pick, spot, snaps, image, outgoing, gathered, hx, hy, sy,
           hs, hr, ss, sr, gs, gr):
    ng, nx, ny = sizes
    shots = checkpoint.shape[0]
    tx, ty, nz = courant.shape
    nrec = positions.shape[2]
    blocks = amplitudes.shape[1] // SNAP
    nh = offsets.shape[0]
    own = nh // ng
    qy = ty // ng
    sub = shots * qy
    groups = tx // qy
    g, a, b = lax.axis_index("grp"), lax.axis_index("gx"), lax.axis_index("gy")
    flip = b % 2
    sign = 1 - 2 * flip
    q = g + flip * (ng - 1 - 2 * g)

    inner_lo, inner_hi = (q > 0).astype(jnp.int32), (q < ng - 1).astype(jnp.int32)
    sides = (
        (a > 0, {"grp": g, "gx": a - 1, "gy": b}),
        (a < nx - 1, {"grp": g, "gx": a + 1, "gy": b}),
        ((q > 0) | (b > 0), {"grp": g - sign * inner_lo, "gx": a, "gy": b - 1 + inner_lo}),
        ((q < ng - 1) | (b < ny - 1), {"grp": g + sign * inner_hi, "gx": a, "gy": b + 1 - inner_hi}),
    )

    barrier = pltpu.get_barrier_semaphore()
    for there, device in sides:
        @pl.when(there)
        def _(device=device):
            pl.semaphore_signal(barrier, inc=1, device_id=device, device_id_type=MESH)
    for step in range(1, ng):
        pl.semaphore_signal(
            barrier, inc=1, device_id={"grp": (g + step) % ng, "gx": a, "gy": b}, device_id_type=MESH
        )

    rows = lax.broadcasted_iota(jnp.int32, (sub, nz), 0)
    lanes = lax.broadcasted_iota(jnp.int32, (sub, nz), 1)
    place = rows % qy
    is_odd = rows * 0 + q % 2 == 1
    first = rows < qy
    half = pl.ds(pl.multiple_of((q // 2) * sub, sub), sub)

    def turn(v, shift, axis=0):
        shift = shift % v.shape[axis]
        return v if shift == 0 else pltpu.roll(v, shift, axis)

    def low(v):
        return jnp.where(is_odd, turn(v, qy), v)

    def high(v):
        return jnp.where(is_odd, v, turn(v, qy))

    def both(v):
        return jnp.where(first, low(v), high(v))

    zero = jnp.zeros((sub, nz), jnp.float32)

    def prepare(x, carry):
        c, e, d = both(courant[x, half, :]), both(epsilon[x, half, :]), both(delta[x, half, :])
        hor[x] = c + 2.0 * c * e
        cpl[x] = c * jnp.sqrt(2.0 * d + 1.0)
        ver[x] = c
        for moment in range(2):
            for field in range(2):
                state[moment, field, 0, x] = jnp.where(
                    first, low(checkpoint[0, moment, field, x, half, :]), high(checkpoint[1, moment, field, x, half, :])
                )
                state[moment, field, 1, x] = zero
        return carry

    lax.fori_loop(0, tx, prepare, 0)

    def pack(side, r, slot, source):
        for m in range(groups):
            packed = None
            for i in range(qy):
                tile = turn(source(m * qy + i), i if side == 0 else i - (qy - 1))
                packed = tile if packed is None else jnp.where(place == i, tile, packed)
            sy[slot, side, r, m] = packed

    for r in range(2):
        for side in range(2):
            pack(side, r, 0, lambda x: state[0, 0, r, x])

    for side in range(2):
        for slot in range(2):
            @pl.when(jnp.logical_not(sides[side][0]))
            def _(slot=slot, side=side):
                hx[slot, side] = jnp.zeros(hx.shape[2:], jnp.float32)

            @pl.when(jnp.logical_not(sides[2 + side][0]))
            def _(slot=slot, side=side):
                hy[slot, side] = jnp.zeros(hy.shape[2:], jnp.float32)

    total = ng - 1
    for there, _ in sides:
        total = total + there.astype(jnp.int32)
    pl.semaphore_wait(barrier, total)

    def halo_copy(slot, side):
        if side < 2:
            source, target = state.at[slot, 0, :, 0 if side == 0 else tx - 1], hx.at[slot, 1 - side]
        else:
            source, target = sy.at[slot, side - 2], hy.at[slot, 3 - side]
        return pltpu.make_async_remote_copy(
            src_ref=source, dst_ref=target, send_sem=hs.at[slot, side], recv_sem=hr.at[slot, side ^ 1],
            device_id=sides[side][1], device_id_type=MESH,
        )

    def halo_arrival(slot, side):
        target = hx.at[slot, side] if side < 2 else hy.at[slot, side - 2]
        return pltpu.make_async_remote_copy(
            src_ref=target, dst_ref=target, send_sem=hs.at[slot, side], recv_sem=hr.at[slot, side],
            device_id=sides[side][1], device_id_type=MESH,
        )

    def snap_copy(j, side, arrival=False):
        source = pl.ds(HMAX, HMAX) if side == 0 else pl.ds(tx, HMAX)
        target = pl.ds(HMAX + tx, HMAX) if side == 0 else pl.ds(0, HMAX)
        if arrival:
            source = target = pl.ds(0, HMAX) if side == 0 else pl.ds(HMAX + tx, HMAX)
        return pltpu.make_async_remote_copy(
            src_ref=snaps.at[j, :, source], dst_ref=snaps.at[j, :, target], send_sem=ss.at[j, side],
            recv_sem=sr.at[j, side if arrival else side ^ 1], device_id=sides[side][1], device_id_type=MESH,
        )

    def send_halos(slot):
        for side in (2, 3, 0, 1):
            @pl.when(sides[side][0])
            def _(side=side):
                halo_copy(slot, side).start()

    def wait_halos(slot):
        for side in range(4):
            @pl.when(sides[side][0])
            def _(side=side):
                halo_arrival(slot, side).wait_recv()
                halo_copy(slot, side).wait_send()

    def send_snap(j):
        for side in range(2):
            @pl.when(sides[side][0])
            def _(side=side):
                snap_copy(j, side).start()

    def wait_snap(j):
        for side in range(2):
            @pl.when(sides[side][0])
            def _(side=side):
                snap_copy(j, side, True).wait_recv()
                snap_copy(j, side).wait_send()

    send_halos(0)

    column = lax.broadcasted_iota(jnp.int32, (tx * sub, nrec), 0)
    level = lax.broadcasted_iota(jnp.int32, (nz, nrec), 0)
    for r in range(2):
        for s in range(shots):
            px = positions[2 * s + r, 0:1, :] - a * tx
            py = positions[2 * s + r, 1:2, :] - (b * ty + q * qy)
            pz = positions[2 * s + r, 2:3, :]
            inside = (px >= 0) & (px < tx) & (py >= 0) & (py < qy)
            cell = jnp.where(inside, px * sub + s * qy + py, -1)
            points = pl.ds(s * nrec, nrec)
            pick[r, :, points] = jnp.where(column == cell, 1.0, 0.0)
            spot[r, points, :] = jnp.where(level == pz, 1.0, 0.0).T.astype(jnp.bfloat16)

    def clear(k, carry):
        for x in range(tx):
            image[k, x] = zero
        return carry

    lax.fori_loop(0, nh, clear, 0)
    for side in range(2):
        @pl.when(jnp.logical_not(sides[side][0]))
        def _(side=side):
            def blank(j, carry):
                for r in range(2):
                    for x in range(HMAX):
                        snaps[j, r, side * (HMAX + tx) + x] = zero
                return carry

            lax.fori_loop(0, blocks, blank, 0)

    def inject(moment):
        for r in range(2):
            found = None
            for s in range(shots):
                points = pl.ds(s * nrec, nrec)
                strength = amplitudes[2 * s + r, pl.ds(moment, 1), :]
                spread = pick[r, :, points] * strength
                upper = spread.astype(jnp.bfloat16)
                lower = (spread - upper.astype(jnp.float32)).astype(jnp.bfloat16)
                for part in (upper, lower):
                    term = jnp.dot(part, spot[r, points, :], preferred_element_type=jnp.float32)
                    found = term if found is None else found + term
            inj[r] = found

    def advance(p):
        for r in range(2):
            for x in range(tx):
                m, w = state[p, 0, r, x], state[p, 1, r, x]
                across = (
                    jnp.where(place == 0, 0.0, turn(m, 1))
                    + jnp.where(place == qy - 1, 0.0, turn(m, -1))
                    - 4.0 * m
                )
                if x > 0:
                    across = across + state[p, 0, r, x - 1]
                if x < tx - 1:
                    across = across + state[p, 0, r, x + 1]
                down = (
                    jnp.where(lanes == 0, 0.0, turn(w, 1, 1))
                    + jnp.where(lanes == nz - 1, 0.0, turn(w, -1, 1))
                    - 2.0 * w
                )
                source = inj[r, pl.ds(x * sub, sub), :]
                coupling = cpl[x]
                state[1 - p, 0, r, x] = 2.0 * m - state[1 - p, 0, r, x] + hor[x] * across + coupling * down + source
                state[1 - p, 1, r, x] = 2.0 * w - state[1 - p, 1, r, x] + coupling * across + ver[x] * down + source

    def repair(p, j):
        for r in range(2):
            for m in range(groups):
                below, above = hy[p, 0, r, m], hy[p, 1, r, m]
                packed = [None, None]
                for i in range(qy):
                    x = m * qy + i
                    extra = jnp.where(place == 0, turn(below, -i), 0.0)
                    extra = jnp.where(place == qy - 1, turn(above, qy - 1 - i), extra)
                    if x == 0:
                        extra = extra + hx[p, 0, r]
                    if x == tx - 1:
                        extra = extra + hx[p, 1, r]
                    main = state[1 - p, 0, r, x] + hor[x] * extra
                    state[1 - p, 0, r, x] = main
                    state[1 - p, 1, r, x] = state[1 - p, 1, r, x] + cpl[x] * extra
                    for side in range(2):
                        tile = turn(main, i if side == 0 else i - (qy - 1))
                        packed[side] = tile if i == 0 else jnp.where(place == i, tile, packed[side])
                    if j is not None:
                        snaps[j, r, HMAX + x] = main
                for side in range(2):
                    sy[1 - p, side, r, m] = packed[side]

    def correlate(j):
        def one(k, carry):
            shift = offsets[k]
            for x in range(tx):
                image[k, x] = image[k, x] + snaps[j, 0, HMAX - shift + x] * snaps[j, 1, HMAX + shift + x]
            return carry

        lax.fori_loop(0, nh, one, 0)

    def block(j, carry):
        for i in range(SNAP):
            p = i % 2
            if i == 0:
                @pl.when(j > 0)
                def _():
                    send_halos(p)
                    send_snap(j - 1)
            else:
                send_halos(p)
            inject(j * SNAP + i)
            advance(p)
            if i == 2:
                @pl.when(j > 0)
                def _():
                    wait_snap(j - 1)
                    correlate(j - 1)
            wait_halos(p)
            repair(p, j if i == SNAP - 1 else None)
        return carry

    lax.fori_loop(0, blocks, block, 0)
    send_snap(blocks - 1)
    wait_snap(blocks - 1)

    def peer_copy(d, arrival=False):
        return pltpu.make_async_remote_copy(
            src_ref=outgoing.at[d], dst_ref=gathered.at[d if arrival else g], send_sem=gs.at[d],
            recv_sem=gr.at[d if arrival else g],
            device_id={"grp": d, "gx": a, "gy": b}, device_id_type=MESH,
        )

    def finish(d, target):
        def pair(n, carry):
            for x in range(tx):
                tiles = []
                for c in range(2):
                    k = d * own + 2 * n + c
                    shift = offsets[k]
                    tile = image[k, x] + snaps[blocks - 1, 0, HMAX - shift + x] * snaps[blocks - 1, 1, HMAX + shift + x]
                    tiles.append(tile + turn(tile, qy))
                target[n, x] = jnp.where(first, tiles[0], tiles[1])
            return carry

        lax.fori_loop(0, own // 2, pair, 0)

    for step in range(1, ng):
        d = (g + step) % ng
        finish(d, outgoing.at[d])
        peer_copy(d).start()
    finish(g, gathered.at[g])
    for step in range(1, ng):
        d = (g + step) % ng
        peer_copy(d, True).wait_recv()
        peer_copy(d).wait_send()

    def place_out(x, carry):
        for h in range(ng // 2):
            left, right = 2 * h, 2 * h + 1
            one = left + flip * (ng - 1 - 2 * left)
            two = right + flip * (ng - 1 - 2 * right)
            for n in range(own // 2):
                u, v = gathered[one, n, x], gathered[two, n, x]
                out[2 * n, x, pl.ds(h * sub, sub), :] = jnp.where(first, u, turn(v, qy))
                out[2 * n + 1, x, pl.ds(h * sub, sub), :] = jnp.where(first, turn(u, qy), v)
        return carry

    lax.fori_loop(0, tx, place_out, 0)


def shards(sizes, checkpoint, courant, epsilon, delta, positions, amplitudes, offsets):
    ng, nx, ny = sizes
    shots = checkpoint.shape[0]
    tx, ty, nz = courant.shape
    nrec = positions.shape[2]
    blocks = amplitudes.shape[1] // SNAP
    nh = offsets.shape[0]
    own = nh // ng
    qy = ty // ng
    sub = shots * qy
    groups = tx // qy
    assert shots == 2 and sub == 8 and ng % 2 == 0 and own % 2 == 0 and tx % qy == 0 and tx >= HMAX
    f32 = jnp.float32
    dma = pltpu.SemaphoreType.DMA
    vmem = pl.BlockSpec(memory_space=pltpu.VMEM)
    return pl.pallas_call(
        functools.partial(kernel, sizes),
        out_shape=jax.ShapeDtypeStruct((own, tx, ty, nz), f32),
        in_specs=[vmem] * 6 + [pl.BlockSpec(memory_space=pltpu.SMEM)],
        out_specs=vmem,
        scratch_shapes=[
            pltpu.VMEM((2, 2, 2, tx, sub, nz), f32),
            pltpu.VMEM((tx, sub, nz), f32),
            pltpu.VMEM((tx, sub, nz), f32),
            pltpu.VMEM((tx, sub, nz), f32),
            pltpu.VMEM((2, tx * sub, nz), f32),
            pltpu.VMEM((2, tx * sub, shots * nrec), f32),
            pltpu.VMEM((2, shots * nrec, nz), jnp.bfloat16),
            pltpu.VMEM((blocks, 2, tx + 2 * HMAX, sub, nz), f32),
            pltpu.VMEM((nh, tx, sub, nz), f32),
            pltpu.VMEM((ng, own // 2, tx, sub, nz), f32),
            pltpu.VMEM((ng, own // 2, tx, sub, nz), f32),
            pltpu.VMEM((2, 2, 2, sub, nz), f32),
            pltpu.VMEM((2, 2, 2, groups, sub, nz), f32),
            pltpu.VMEM((2, 2, 2, groups, sub, nz), f32),
            dma((2, 4)),
            dma((2, 4)),
            dma((blocks, 2)),
            dma((blocks, 2)),
            dma((ng,)),
            dma((ng,)),
        ],
        compiler_params=pltpu.CompilerParams(
            collective_id=0, has_side_effects=True, vmem_limit_bytes=56 * 1024 * 1024
        ),
    )(courant, epsilon, delta, checkpoint, positions, amplitudes, offsets)


def solution(mesh):
    sizes = tuple(mesh.shape[axis] for axis in ("grp", "gx", "gy"))
    return jax.shard_map(
        functools.partial(shards, sizes),
        mesh=mesh,
        in_specs=(
            P(None, None, None, "gx", "gy", None),
            P("gx", "gy", None),
            P("gx", "gy", None),
            P("gx", "gy", None),
            P(),
            P(),
            P(),
        ),
        out_specs=P("grp", "gx", "gy", None),
        check_vma=False,
    )
```

time: 396 us -> 95.5 us (0.24)
  the two profiles are of different devices: /device:TPU:0 before, /device:TPU:24 now
where the time goes in v1:
time: 95.5 us; the launch traced here: 95.2 us
  Pallas kernels  91.6 us (96%)
  local copies, waits for them, and re-layouts  3.63 us (4%)
    pallas_call x1, Pallas kernels, shards(): pl.pallas_call(functools.partial(kernel, sizes), out_shape=jax.ShapeDtype...  91.6 us
    unnamed x2, local copies, waits for them, and re-layouts  3.63 us

profile of v1, /device:TPU:24, one launch (start us, length us, event | category | flops | bytes accessed | tf_op | source)
XLA Modules:
  0.0 95.2 jit_solution(10630873235782091392)
XLA Ops:
  0.0 1.4 %copy.8.positions = s32[4,3,512]{2,1,0:T(4,128)} copy(s32[4,3,512]{2,0,1:T(4,128)} %param.11) | data formatting | bytes 49152 | tf_op args[4]
  1.4 91.6 %shard_map.73 = f32[4,16,16,256]{3,2,1,0:T(8,128)} custom-call(f32[16,16,256]{2,1,0:T(8,128)} %courant.1, f32[16,16,256]{2,1,0:T(8,128)} %epsilon.1, f32[16,16,256]{2,1,0:T(8,128)} %delta.1, f32[2,2,2,16,16,256]{5,4,3,2,1,0:T(8,128)} %checkpoint.1, s32[4,3,512]{2,1,0:T(4,128)} %copy.8.positions, f32[4,16,512]{2,1,0:T(8,128)} %amplitudes.1, s32[16]{0:T(128)} %offsets.1), custom_call_target="tpu_custom_call" | custom-call | tf_op jit(solution)/shard_map/pallas_call | solution.py:354
  93.0 2.3 %copy.10 = f32[4,16,16,256]{3,2,1,0:T(8,128)} copy(f32[4,16,16,256]{3,2,1,0:T(8,128)} %shard_map.73) | data formatting | bytes 2097152

commit v2 on v1

--- a/solution.py
+++ b/solution.py
@@ -1,4 +1,5 @@
 import functools
+import math
 import jax
 import jax.numpy as jnp
 from jax import lax
@@ -11,8 +12,8 @@
 MESH = pl.DeviceIdType.MESH
 
 
-def kernel(sizes, courant, epsilon, delta, checkpoint, positions, amplitudes, offsets, out,
-           state, hor, cpl, ver, inj, pick, spot, snaps, image, outgoing, gathered, hx, hy, sy,
+def kernel(sizes, courant, epsilon, delta, checkpoint, positions, amplitudes, offsets, gathered,
+           state, hor, cpl, ver, inj, pick, spot, snaps, image, outgoing, hx, hy, sy,
            hs, hr, ss, sr, gs, gr):
     ng, nx, ny = sizes
     shots = checkpoint.shape[0]
@@ -111,68 +112,70 @@
         total = total + there.astype(jnp.int32)
     pl.semaphore_wait(barrier, total)
 
-    def halo_copy(slot, side):
+    def halo_copy(slot, r, side):
         if side < 2:
-            source, target = state.at[slot, 0, :, 0 if side == 0 else tx - 1], hx.at[slot, 1 - side]
+            source, target = state.at[slot, 0, r, 0 if side == 0 else tx - 1], hx.at[slot, 1 - side, r]
         else:
-            source, target = sy.at[slot, side - 2], hy.at[slot, 3 - side]
+            source, target = sy.at[slot, side - 2, r], hy.at[slot, 3 - side, r]
         return pltpu.make_async_remote_copy(
-            src_ref=source, dst_ref=target, send_sem=hs.at[slot, side], recv_sem=hr.at[slot, side ^ 1],
+            src_ref=source, dst_ref=target, send_sem=hs.at[slot, r, side], recv_sem=hr.at[slot, r, side ^ 1],
             device_id=sides[side][1], device_id_type=MESH,
         )
 
-    def halo_arrival(slot, side):
-        target = hx.at[slot, side] if side < 2 else hy.at[slot, side - 2]
+    def halo_arrival(slot, r, side):
+        target = hx.at[slot, side, r] if side < 2 else hy.at[slot, side - 2, r]
         return pltpu.make_async_remote_copy(
-            src_ref=target, dst_ref=target, send_sem=hs.at[slot, side], recv_sem=hr.at[slot, side],
+            src_ref=target, dst_ref=target, send_sem=hs.at[slot, r, side], recv_sem=hr.at[slot, r, side],
             device_id=sides[side][1], device_id_type=MESH,
         )
 
-    def snap_copy(j, side, arrival=False):
+    def snap_copy(j, r, side, arrival=False):
         source = pl.ds(HMAX, HMAX) if side == 0 else pl.ds(tx, HMAX)
         target = pl.ds(HMAX + tx, HMAX) if side == 0 else pl.ds(0, HMAX)
         if arrival:
             source = target = pl.ds(0, HMAX) if side == 0 else pl.ds(HMAX + tx, HMAX)
         return pltpu.make_async_remote_copy(
-            src_ref=snaps.at[j, :, source], dst_ref=snaps.at[j, :, target], send_sem=ss.at[j, side],
-            recv_sem=sr.at[j, side if arrival else side ^ 1], device_id=sides[side][1], device_id_type=MESH,
+            src_ref=snaps.at[j, r, source], dst_ref=snaps.at[j, r, target], send_sem=ss.at[j, r, side],
+            recv_sem=sr.at[j, r, side if arrival else side ^ 1], device_id=sides[side][1], device_id_type=MESH,
         )
 
-    def send_halos(slot):
+    def send_halos(slot, r):
         for side in (2, 3, 0, 1):
             @pl.when(sides[side][0])
             def _(side=side):
-                halo_copy(slot, side).start()
-
-    def wait_halos(slot):
+                halo_copy(slot, r, side).start()
+
+    def wait_halos(slot, r):
         for side in range(4):
             @pl.when(sides[side][0])
             def _(side=side):
-                halo_arrival(slot, side).wait_recv()
-                halo_copy(slot, side).wait_send()
-
-    def send_snap(j):
+                halo_arrival(slot, r, side).wait_recv()
+                halo_copy(slot, r, side).wait_send()
+
+    def send_snap(j, r):
         for side in range(2):
             @pl.when(sides[side][0])
             def _(side=side):
-                snap_copy(j, side).start()
+                snap_copy(j, r, side).start()
 
     def wait_snap(j):
-        for side in range(2):
-            @pl.when(sides[side][0])
-            def _(side=side):
-                snap_copy(j, side, True).wait_recv()
-                snap_copy(j, side).wait_send()
-
-    send_halos(0)
+        for r in range(2):
+            for side in range(2):
+                @pl.when(sides[side][0])
+                def _(r=r, side=side):
+                    snap_copy(j, r, side, True).wait_recv()
+                    snap_copy(j, r, side).wait_send()
+
+    send_halos(0, 0)
+    send_halos(0, 1)
 
     column = lax.broadcasted_iota(jnp.int32, (tx * sub, nrec), 0)
     level = lax.broadcasted_iota(jnp.int32, (nz, nrec), 0)
     for r in range(2):
         for s in range(shots):
-            px = positions[2 * s + r, 0:1, :] - a * tx
-            py = positions[2 * s + r, 1:2, :] - (b * ty + q * qy)
-            pz = positions[2 * s + r, 2:3, :]
+            px = positions[0, 2 * s + r : 2 * s + r + 1, :] - a * tx
+            py = positions[1, 2 * s + r : 2 * s + r + 1, :] - (b * ty + q * qy)
+            pz = positions[2, 2 * s + r : 2 * s + r + 1, :]
             inside = (px >= 0) & (px < tx) & (py >= 0) & (py < qy)
             cell = jnp.where(inside, px * sub + s * qy + py, -1)
             points = pl.ds(s * nrec, nrec)
@@ -196,66 +199,63 @@
 
             lax.fori_loop(0, blocks, blank, 0)
 
-    def inject(moment):
-        for r in range(2):
-            found = None
-            for s in range(shots):
-                points = pl.ds(s * nrec, nrec)
-                strength = amplitudes[2 * s + r, pl.ds(moment, 1), :]
-                spread = pick[r, :, points] * strength
-                upper = spread.astype(jnp.bfloat16)
-                lower = (spread - upper.astype(jnp.float32)).astype(jnp.bfloat16)
-                for part in (upper, lower):
-                    term = jnp.dot(part, spot[r, points, :], preferred_element_type=jnp.float32)
-                    found = term if found is None else found + term
-            inj[r] = found
-
-    def advance(p):
-        for r in range(2):
-            for x in range(tx):
-                m, w = state[p, 0, r, x], state[p, 1, r, x]
-                across = (
-                    jnp.where(place == 0, 0.0, turn(m, 1))
-                    + jnp.where(place == qy - 1, 0.0, turn(m, -1))
-                    - 4.0 * m
-                )
-                if x > 0:
-                    across = across + state[p, 0, r, x - 1]
-                if x < tx - 1:
-                    across = across + state[p, 0, r, x + 1]
-                down = (
-                    jnp.where(lanes == 0, 0.0, turn(w, 1, 1))
-                    + jnp.where(lanes == nz - 1, 0.0, turn(w, -1, 1))
-                    - 2.0 * w
-                )
-                source = inj[r, pl.ds(x * sub, sub), :]
-                coupling = cpl[x]
-                state[1 - p, 0, r, x] = 2.0 * m - state[1 - p, 0, r, x] + hor[x] * across + coupling * down + source
-                state[1 - p, 1, r, x] = 2.0 * w - state[1 - p, 1, r, x] + coupling * across + ver[x] * down + source
-
-    def repair(p, j):
-        for r in range(2):
-            for m in range(groups):
-                below, above = hy[p, 0, r, m], hy[p, 1, r, m]
-                packed = [None, None]
-                for i in range(qy):
-                    x = m * qy + i
-                    extra = jnp.where(place == 0, turn(below, -i), 0.0)
-                    extra = jnp.where(place == qy - 1, turn(above, qy - 1 - i), extra)
-                    if x == 0:
-                        extra = extra + hx[p, 0, r]
-                    if x == tx - 1:
-                        extra = extra + hx[p, 1, r]
-                    main = state[1 - p, 0, r, x] + hor[x] * extra
-                    state[1 - p, 0, r, x] = main
-                    state[1 - p, 1, r, x] = state[1 - p, 1, r, x] + cpl[x] * extra
-                    for side in range(2):
-                        tile = turn(main, i if side == 0 else i - (qy - 1))
-                        packed[side] = tile if i == 0 else jnp.where(place == i, tile, packed[side])
-                    if j is not None:
-                        snaps[j, r, HMAX + x] = main
+    def inject(moment, r):
+        found = None
+        for s in range(shots):
+            points = pl.ds(s * nrec, nrec)
+            strength = amplitudes[2 * s + r, pl.ds(moment, 1), :]
+            spread = pick[r, :, points] * strength
+            upper = spread.astype(jnp.bfloat16)
+            lower = (spread - upper.astype(jnp.float32)).astype(jnp.bfloat16)
+            for part in (upper, lower):
+                term = jnp.dot(part, spot[r, points, :], preferred_element_type=jnp.float32)
+                found = term if found is None else found + term
+        inj[r] = found
+
+    def advance(p, r):
+        for x in range(tx):
+            m, w = state[p, 0, r, x], state[p, 1, r, x]
+            across = (
+                jnp.where(place == 0, 0.0, turn(m, 1))
+                + jnp.where(place == qy - 1, 0.0, turn(m, -1))
+                - 4.0 * m
+            )
+            if x > 0:
+                across = across + state[p, 0, r, x - 1]
+            if x < tx - 1:
+                across = across + state[p, 0, r, x + 1]
+            down = (
+                jnp.where(lanes == 0, 0.0, turn(w, 1, 1))
+                + jnp.where(lanes == nz - 1, 0.0, turn(w, -1, 1))
+                - 2.0 * w
+            )
+            source = inj[r, pl.ds(x * sub, sub), :]
+            coupling = cpl[x]
+            state[1 - p, 0, r, x] = 2.0 * m - state[1 - p, 0, r, x] + hor[x] * across + coupling * down + source
+            state[1 - p, 1, r, x] = 2.0 * w - state[1 - p, 1, r, x] + coupling * across + ver[x] * down + source
+
+    def repair(p, r, j):
+        for m in range(groups):
+            below, above = hy[p, 0, r, m], hy[p, 1, r, m]
+            packed = [None, None]
+            for i in range(qy):
+                x = m * qy + i
+                extra = jnp.where(place == 0, turn(below, -i), 0.0)
+                extra = jnp.where(place == qy - 1, turn(above, qy - 1 - i), extra)
+                if x == 0:
+                    extra = extra + hx[p, 0, r]
+                if x == tx - 1:
+                    extra = extra + hx[p, 1, r]
+                main = state[1 - p, 0, r, x] + hor[x] * extra
+                state[1 - p, 0, r, x] = main
+                state[1 - p, 1, r, x] = state[1 - p, 1, r, x] + cpl[x] * extra
                 for side in range(2):
-                    sy[1 - p, side, r, m] = packed[side]
+                    tile = turn(main, i if side == 0 else i - (qy - 1))
+                    packed[side] = tile if i == 0 else jnp.where(place == i, tile, packed[side])
+                if j is not None:
+                    snaps[j, r, HMAX + x] = main
+            for side in range(2):
+                sy[1 - p, side, r, m] = packed[side]
 
     def correlate(j):
         def one(k, carry):
@@ -269,26 +269,33 @@
     def block(j, carry):
         for i in range(SNAP):
             p = i % 2
-            if i == 0:
-                @pl.when(j > 0)
-                def _():
-                    send_halos(p)
-                    send_snap(j - 1)
-            else:
-                send_halos(p)
-            inject(j * SNAP + i)
-            advance(p)
-            if i == 2:
-                @pl.when(j > 0)
-                def _():
-                    wait_snap(j - 1)
-                    correlate(j - 1)
-            wait_halos(p)
-            repair(p, j if i == SNAP - 1 else None)
+            for r in range(2):
+                inject(j * SNAP + i, r)
+                advance(p, r)
+                if i == 2 and r == 0:
+                    @pl.when(j > 0)
+                    def _():
+                        wait_snap(j - 1)
+                        correlate(j - 1)
+                wait_halos(p, r)
+                repair(p, r, j if i == SNAP - 1 else None)
+                if i == SNAP - 1:
+                    @pl.when(j < blocks - 1)
+                    def _():
+                        send_halos(1 - p, r)
+
+                    @pl.when(j == blocks - 1)
+                    def _():
+                        send_snap(j, r)
+                else:
+                    send_halos(1 - p, r)
+                if i == 0:
+                    @pl.when(j > 0)
+                    def _():
+                        send_snap(j - 1, r)
         return carry
 
     lax.fori_loop(0, blocks, block, 0)
-    send_snap(blocks - 1)
     wait_snap(blocks - 1)
 
     def peer_copy(d, arrival=False):
@@ -322,18 +329,21 @@
         peer_copy(d, True).wait_recv()
         peer_copy(d).wait_send()
 
-    def place_out(x, carry):
-        for h in range(ng // 2):
-            left, right = 2 * h, 2 * h + 1
-            one = left + flip * (ng - 1 - 2 * left)
-            two = right + flip * (ng - 1 - 2 * right)
-            for n in range(own // 2):
+
+def place(gathered, out):
+    ng, pairs, span, sub, nz = gathered.shape
+    flip = lax.axis_index("gy") % 2
+    qy = sub // 2
+    first = lax.broadcasted_iota(jnp.int32, (sub, nz), 0) < qy
+    for h in range(ng // 2):
+        left, right = 2 * h, 2 * h + 1
+        one = left + flip * (ng - 1 - 2 * left)
+        two = right + flip * (ng - 1 - 2 * right)
+        for n in range(pairs):
+            for x in range(span):
                 u, v = gathered[one, n, x], gathered[two, n, x]
-                out[2 * n, x, pl.ds(h * sub, sub), :] = jnp.where(first, u, turn(v, qy))
-                out[2 * n + 1, x, pl.ds(h * sub, sub), :] = jnp.where(first, turn(u, qy), v)
-        return carry
-
-    lax.fori_loop(0, tx, place_out, 0)
+                out[2 * n, x, pl.ds(h * sub, sub), :] = jnp.where(first, u, pltpu.roll(v, qy, 0))
+                out[2 * n + 1, x, pl.ds(h * sub, sub), :] = jnp.where(first, pltpu.roll(u, qy, 0), v)
 
 
 def shards(sizes, checkpoint, courant, epsilon, delta, positions, amplitudes, offsets):
@@ -351,9 +361,9 @@
     f32 = jnp.float32
     dma = pltpu.SemaphoreType.DMA
     vmem = pl.BlockSpec(memory_space=pltpu.VMEM)
-    return pl.pallas_call(
+    gathered = pl.pallas_call(
         functools.partial(kernel, sizes),
-        out_shape=jax.ShapeDtypeStruct((own, tx, ty, nz), f32),
+        out_shape=jax.ShapeDtypeStruct((ng, own // 2, tx, sub, nz), f32),
         in_specs=[vmem] * 6 + [pl.BlockSpec(memory_space=pltpu.SMEM)],
         out_specs=vmem,
         scratch_shapes=[
@@ -367,21 +377,29 @@
             pltpu.VMEM((blocks, 2, tx + 2 * HMAX, sub, nz), f32),
             pltpu.VMEM((nh, tx, sub, nz), f32),
             pltpu.VMEM((ng, own // 2, tx, sub, nz), f32),
-            pltpu.VMEM((ng, own // 2, tx, sub, nz), f32),
             pltpu.VMEM((2, 2, 2, sub, nz), f32),
             pltpu.VMEM((2, 2, 2, groups, sub, nz), f32),
             pltpu.VMEM((2, 2, 2, groups, sub, nz), f32),
-            dma((2, 4)),
-            dma((2, 4)),
-            dma((blocks, 2)),
-            dma((blocks, 2)),
+            dma((2, 2, 4)),
+            dma((2, 2, 4)),
+            dma((blocks, 2, 2)),
+            dma((blocks, 2, 2)),
             dma((ng,)),
             dma((ng,)),
         ],
         compiler_params=pltpu.CompilerParams(
             collective_id=0, has_side_effects=True, vmem_limit_bytes=56 * 1024 * 1024
         ),
-    )(courant, epsilon, delta, checkpoint, positions, amplitudes, offsets)
+    )(courant, epsilon, delta, checkpoint, positions.transpose(1, 0, 2), amplitudes, offsets)
+    cut = math.gcd(tx, 4)
+    span = tx // cut
+    return pl.pallas_call(
+        place,
+        grid=(cut,),
+        out_shape=jax.ShapeDtypeStruct((own, tx, ty, nz), f32),
+        in_specs=[pl.BlockSpec((ng, own // 2, span, sub, nz), lambda n: (0, 0, n, 0, 0))],
+        out_specs=pl.BlockSpec((own, span, ty, nz), lambda n: (0, n, 0, 0)),
+    )(gathered)
 
 
 def solution(mesh):

time: 95.5 us -> 89.6 us (0.938)
  local copies, waits for them, and re-layouts: 3.63 us -> 0 us
  Pallas kernels: 91.6 us -> 89.4 us
    pallas_call x1, Pallas kernels: 91.6 us -> 86 us  [shards(): pl.pallas_call(functools.partial(kernel, sizes), out_shape=jax.ShapeDtype...]
    unnamed x2 -> x0, local copies, waits for them, and re-layouts: 3.63 us -> none
    pallas_call x0 -> x1, Pallas kernels: none -> 3.39 us  [shards(): pl.pallas_call(place, grid=(cut,), out_shape=jax.ShapeDtypeStruct((own, t...]
where the time goes in v2:
time: 89.6 us; the launch traced here: 89.4 us
  Pallas kernels  89.4 us (100%)
    pallas_call x1, Pallas kernels, shards(): pl.pallas_call(functools.partial(kernel, sizes), out_shape=jax.ShapeDtype...  86 us
    pallas_call x1, Pallas kernels, shards(): pl.pallas_call(place, grid=(cut,), out_shape=jax.ShapeDtypeStruct((own, t...  3.39 us

profile of v2, /device:TPU:24, one launch (start us, length us, event | category | flops | bytes accessed | tf_op | source)
XLA Modules:
  0.0 89.4 jit_solution(2778510235227540715)
XLA Ops:
  0.0 86.0 %shard_map.73.gathered = f32[4,2,16,8,256]{4,3,2,1,0:T(8,128)} custom-call(f32[16,16,256]{2,1,0:T(8,128)} %courant.1, f32[16,16,256]{2,1,0:T(8,128)} %epsilon.1, f32[16,16,256]{2,1,0:T(8,128)} %delta.1, f32[2,2,2,16,16,256]{5,4,3,2,1,0:T(8,128)} %checkpoint.1, s32[3,4,512]{2,1,0:T(4,128)} %bitcast.1, f32[4,16,512]{2,1,0:T(8,128)} %amplitudes.1, s32[16]{0:T(128)} %offsets.1), custom_call_target="tpu_custom_call" | custom-call | tf_op jit(solution)/shard_map/pallas_call | solution.py:364
  86.0 3.4 %shard_map.74 = f32[4,16,16,256]{3,2,1,0:T(8,128)} custom-call(f32[4,2,16,8,256]{4,3,2,1,0:T(8,128)} %shard_map.73.gathered), custom_call_target="tpu_custom_call" | custom-call | tf_op jit(solution)/shard_map/pallas_call | solution.py:396

commit v3 on v2

--- a/solution.py
+++ b/solution.py
@@ -179,7 +179,7 @@
             inside = (px >= 0) & (px < tx) & (py >= 0) & (py < qy)
             cell = jnp.where(inside, px * sub + s * qy + py, -1)
             points = pl.ds(s * nrec, nrec)
-            pick[r, :, points] = jnp.where(column == cell, 1.0, 0.0)
+            pick[r, :, points] = jnp.where(column == cell, 1.0, 0.0).astype(jnp.bfloat16)
             spot[r, points, :] = jnp.where(level == pz, 1.0, 0.0).T.astype(jnp.bfloat16)
 
     def clear(k, carry):
@@ -200,17 +200,22 @@
             lax.fori_loop(0, blocks, blank, 0)
 
     def inject(moment, r):
-        found = None
-        for s in range(shots):
-            points = pl.ds(s * nrec, nrec)
-            strength = amplitudes[2 * s + r, pl.ds(moment, 1), :]
-            spread = pick[r, :, points] * strength
-            upper = spread.astype(jnp.bfloat16)
-            lower = (spread - upper.astype(jnp.float32)).astype(jnp.bfloat16)
-            for part in (upper, lower):
-                term = jnp.dot(part, spot[r, points, :], preferred_element_type=jnp.float32)
-                found = term if found is None else found + term
-        inj[r] = found
+        strength = jnp.concatenate(
+            [amplitudes[2 * s + r, pl.ds(moment, 1), :] for s in range(shots)], axis=1
+        )
+        strength = jnp.broadcast_to(strength, (2 * sub, shots * nrec))
+        upper = strength.astype(jnp.bfloat16)
+        lower = (strength - upper.astype(jnp.float32)).astype(jnp.bfloat16)
+        spread = jnp.concatenate(
+            [
+                pick[r, pl.ds(2 * sub * m, 2 * sub), :] * part
+                for part in (upper, lower)
+                for m in range(tx // 2)
+            ],
+            axis=0,
+        )
+        found = jnp.dot(spread, spot[r], preferred_element_type=jnp.float32)
+        inj[r] = found[: tx * sub] + found[tx * sub :]
 
     def advance(p, r):
         for x in range(tx):
@@ -357,7 +362,7 @@
     qy = ty // ng
     sub = shots * qy
     groups = tx // qy
-    assert shots == 2 and sub == 8 and ng % 2 == 0 and own % 2 == 0 and tx % qy == 0 and tx >= HMAX
+    assert shots == 2 and sub == 8 and ng % 2 == 0 and own % 2 == 0 and tx % qy == 0 and tx >= HMAX and tx % 2 == 0
     f32 = jnp.float32
     dma = pltpu.SemaphoreType.DMA
     vmem = pl.BlockSpec(memory_space=pltpu.VMEM)
@@ -372,7 +377,7 @@
             pltpu.VMEM((tx, sub, nz), f32),
             pltpu.VMEM((tx, sub, nz), f32),
             pltpu.VMEM((2, tx * sub, nz), f32),
-            pltpu.VMEM((2, tx * sub, shots * nrec), f32),
+            pltpu.VMEM((2, tx * sub, shots * nrec), jnp.bfloat16),
             pltpu.VMEM((2, shots * nrec, nz), jnp.bfloat16),
             pltpu.VMEM((blocks, 2, tx + 2 * HMAX, sub, nz), f32),
             pltpu.VMEM((nh, tx, sub, nz), f32),

time: 89.6 us -> 89.6 us (level)
  no operation moved by 1% of the time
where the time goes in v3:
time: 89.6 us; the launch traced here: 89.4 us
  Pallas kernels  89.4 us (100%)
    pallas_call x1, Pallas kernels, shards(): pl.pallas_call(functools.partial(kernel, sizes), out_shape=jax.ShapeDtype...  86 us
    pallas_call x1, Pallas kernels, shards(): pl.pallas_call(place, grid=(cut,), out_shape=jax.ShapeDtypeStruct((own, t...  3.39 us

profile of v3, /device:TPU:24, one launch (start us, length us, event | category | flops | bytes accessed | tf_op | source)
XLA Modules:
  0.0 89.4 jit_solution(8255529199517426087)
XLA Ops:
  0.0 86.0 %shard_map.73.gathered = f32[4,2,16,8,256]{4,3,2,1,0:T(8,128)} custom-call(f32[16,16,256]{2,1,0:T(8,128)} %courant.1, f32[16,16,256]{2,1,0:T(8,128)} %epsilon.1, f32[16,16,256]{2,1,0:T(8,128)} %delta.1, f32[2,2,2,16,16,256]{5,4,3,2,1,0:T(8,128)} %checkpoint.1, s32[3,4,512]{2,1,0:T(4,128)} %bitcast.1, f32[4,16,512]{2,1,0:T(8,128)} %amplitudes.1, s32[16]{0:T(128)} %offsets.1), custom_call_target="tpu_custom_call" | custom-call | tf_op jit(solution)/shard_map/pallas_call | solution.py:369
  86.0 3.4 %shard_map.74 = f32[4,16,16,256]{3,2,1,0:T(8,128)} custom-call(f32[4,2,16,8,256]{4,3,2,1,0:T(8,128)} %shard_map.73.gathered), custom_call_target="tpu_custom_call" | custom-call | tf_op jit(solution)/shard_map/pallas_call | solution.py:401

commit v4 on v3

--- a/solution.py
+++ b/solution.py
@@ -13,7 +13,7 @@
 
 
 def kernel(sizes, courant, epsilon, delta, checkpoint, positions, amplitudes, offsets, gathered,
-           state, hor, cpl, ver, inj, pick, spot, snaps, image, outgoing, hx, hy, sy,
+           state, hor, cpl, ver, edge, inj, pick, spot, snaps, image, outgoing, hx, hy, sy,
            hs, hr, ss, sr, gs, gr):
     ng, nx, ny = sizes
     shots = checkpoint.shape[0]
@@ -253,7 +253,7 @@
                     extra = extra + hx[p, 1, r]
                 main = state[1 - p, 0, r, x] + hor[x] * extra
                 state[1 - p, 0, r, x] = main
-                state[1 - p, 1, r, x] = state[1 - p, 1, r, x] + cpl[x] * extra
+                edge[x] = extra
                 for side in range(2):
                     tile = turn(main, i if side == 0 else i - (qy - 1))
                     packed[side] = tile if i == 0 else jnp.where(place == i, tile, packed[side])
@@ -261,6 +261,10 @@
                     snaps[j, r, HMAX + x] = main
             for side in range(2):
                 sy[1 - p, side, r, m] = packed[side]
+
+    def repair_aux(p, r):
+        for x in range(tx):
+            state[1 - p, 1, r, x] = state[1 - p, 1, r, x] + cpl[x] * edge[x]
 
     def correlate(j):
         def one(k, carry):
@@ -298,6 +302,7 @@
                     @pl.when(j > 0)
                     def _():
                         send_snap(j - 1, r)
+                repair_aux(p, r)
         return carry
 
     lax.fori_loop(0, blocks, block, 0)
@@ -373,6 +378,7 @@
         out_specs=vmem,
         scratch_shapes=[
             pltpu.VMEM((2, 2, 2, tx, sub, nz), f32),
+            pltpu.VMEM((tx, sub, nz), f32),
             pltpu.VMEM((tx, sub, nz), f32),
             pltpu.VMEM((tx, sub, nz), f32),
             pltpu.VMEM((tx, sub, nz), f32),

time: 89.6 us -> 89.4 us (level)
  no operation moved by 1% of the time
where the time goes in v4:
time: 89.4 us; the launch traced here: 89.2 us
  Pallas kernels  89.2 us (100%)
    pallas_call x1, Pallas kernels, shards(): pl.pallas_call(functools.partial(kernel, sizes), out_shape=jax.ShapeDtype...  85.8 us
    pallas_call x1, Pallas kernels, shards(): pl.pallas_call(place, grid=(cut,), out_shape=jax.ShapeDtypeStruct((own, t...  3.39 us

profile of v4, /device:TPU:24, one launch (start us, length us, event | category | flops | bytes accessed | tf_op | source)
XLA Modules:
  0.0 89.2 jit_solution(12828253141795375428)
XLA Ops:
  0.0 85.8 %shard_map.73.gathered = f32[4,2,16,8,256]{4,3,2,1,0:T(8,128)} custom-call(f32[16,16,256]{2,1,0:T(8,128)} %courant.1, f32[16,16,256]{2,1,0:T(8,128)} %epsilon.1, f32[16,16,256]{2,1,0:T(8,128)} %delta.1, f32[2,2,2,16,16,256]{5,4,3,2,1,0:T(8,128)} %checkpoint.1, s32[3,4,512]{2,1,0:T(4,128)} %bitcast.1, f32[4,16,512]{2,1,0:T(8,128)} %amplitudes.1, s32[16]{0:T(128)} %offsets.1), custom_call_target="tpu_custom_call" | custom-call | tf_op jit(solution)/shard_map/pallas_call | solution.py:374
  85.8 3.4 %shard_map.74 = f32[4,16,16,256]{3,2,1,0:T(8,128)} custom-call(f32[4,2,16,8,256]{4,3,2,1,0:T(8,128)} %shard_map.73.gathered), custom_call_target="tpu_custom_call" | custom-call | tf_op jit(solution)/shard_map/pallas_call | solution.py:407
